TPU v7x, 512 devices: a whole 4x8x8 slice. The times are simulated.
512 devices in a mesh: rows: 64 (over y, x, core), dates: 8 (over z).
Axes of the slice: x: 4, y: 8, z: 8, core: 2. Of those that a mesh axis runs over, the one named last changes fastest.
Arguments:
- obs_mask: int32 [16, 512, 4096], P('dates', 'rows'), may hold values 0 or 1
- precision: float32 [16, 512, 4096], P('dates', 'rows'), may hold values from 0.5 to 4
- observed: float32 [16, 512, 4096], P('dates', 'rows')
- edge_class: int32 [2, 512, 4096], P(None, 'rows'), may hold values from 0 to 7
- temporal_weight: float32 [15], replicated, may hold values from 0.5 to 4
- inverse: bfloat16 [16, 16, 512, 4096], P(None, None, 'rows', 'dates'), as said below
Outputs:
- solution: float32 [16, 512, 4096], P('dates', 'rows')
- residual: float32 [16, 512, 4096], P('dates', 'rows')
Inputs may be any that keep to these rules, and one draw needn't show every extreme that they name: `inverse`: each pixel's matrix is symmetric with a diagonal larger than the sum of magnitudes of its row's other entries.
All inputs are finite; a program needn't handle non-finite values. No bound on the sum of `obs_mask` on one device may be relied on, other than what follows from the above.
Results may differ from a plain program's by a relative error of at most 0.0065.
Values sent between devices are 32-bit elements; how exact they have to be, the bound alone decides.
A program may use at most 64 MiB of HBM per device.

v0:
```python
import jax
import jax.numpy as jnp
from jax import lax
from jax.sharding import PartitionSpec as P

mass_term = 0.1


def shifted(value, axis, steps):
    count = lax.axis_size(axis)
    first, last = (max(0, -steps), min(count, count - steps))
    return lax.ppermute(value, axis, [(i, i + steps) for i in range(first, last)])


def apply_inverse(inverse, values):
    total = inverse[:, 0].astype(jnp.float32) * values[0][None]
    for source in range(1, values.shape[0]):
        total = total + inverse[:, source].astype(jnp.float32) * values[source][None]
    return total


def body(obs_mask, precision, observed, edge_class, temporal_weight, inverse):
    dates_here, rows_here, columns = observed.shape
    cols_here = inverse.shape[3]
    line_start = lax.axis_index("rows") * rows_here
    lines_total = rows_here * lax.axis_size("rows")
    col_start = lax.axis_index("dates") * cols_here
    weight = obs_mask.astype(jnp.float32) * precision
    both = jnp.stack([weight, weight * observed])
    both = lax.all_to_all(both, "dates", split_axis=3, concat_axis=1, tiled=True)
    weight, rhs = (both[0], both[1])
    classes = 0.25 * (edge_class.astype(jnp.float32) + 1.0)
    col_ids = lax.broadcasted_iota(jnp.int32, (rows_here, columns), 1)
    row_ids = lax.broadcasted_iota(jnp.int32, (rows_here, cols_here), 0) + line_start
    across_all = jnp.where(col_ids == columns - 1, 0.0, classes[0])
    across_ext = jnp.pad(across_all, ((0, 0), (1, 0)))
    across_prev = lax.dynamic_slice_in_dim(across_ext, col_start, cols_here, 1)
    across = lax.dynamic_slice_in_dim(across_all, col_start, cols_here, 1)
    downward = lax.dynamic_slice_in_dim(classes[1], col_start, cols_here, 1)
    downward = jnp.where(row_ids == lines_total - 1, 0.0, downward)
    downward_prev = jnp.concatenate([shifted(downward[-1:], "rows", 1), downward[:-1]], axis=0)
    zero_one = jnp.zeros((1,), jnp.float32)
    tau_up = jnp.concatenate([temporal_weight, zero_one])[:, None, None]
    tau_down = jnp.concatenate([zero_one, temporal_weight])[:, None, None]
    centre = (
        mass_term
        + weight
        + (across + across_prev + downward + downward_prev)[None]
        + (tau_up + tau_down)
    )

    def operator(field):
        above = jnp.concatenate([shifted(field[:, -1:], "rows", 1), field[:, :-1]], axis=1)
        below = jnp.concatenate([field[:, 1:], shifted(field[:, :1], "rows", -1)], axis=1)
        left = jnp.concatenate([shifted(field[:, :, -1:], "dates", 1), field[:, :, :-1]], axis=2)
        right = jnp.concatenate([field[:, :, 1:], shifted(field[:, :, :1], "dates", -1)], axis=2)
        before = jnp.pad(field, ((1, 0), (0, 0), (0, 0)))[:-1]
        after = jnp.pad(field, ((0, 1), (0, 0), (0, 0)))[1:]
        return (
            centre * field
            - (across * right + across_prev * left)
            - (downward * below + downward_prev * above)
            - (tau_up * after + tau_down * before)
        )

    precond = apply_inverse(inverse, rhs)
    image = operator(precond)
    mapped = apply_inverse(inverse, image)
    mapped_image = operator(mapped)
    sums = jnp.stack(
        [
            jnp.sum(rhs * precond),
            jnp.sum(precond * image),
            jnp.sum(image * mapped),
            jnp.sum(mapped * mapped_image),
        ]
    )
    sums = lax.psum(sums, ("rows", "dates"))
    rz, dd, ee, ff = (sums[0], sums[1], sums[2], sums[3])
    alpha = rz / dd
    grown = alpha * ee / dd
    alpha_next = (alpha * alpha * ee - rz) / (alpha * alpha * (ff - ee * ee / dd))
    first = alpha + alpha_next * grown
    second = alpha_next * alpha
    out = jnp.stack(
        [first * precond - second * mapped, rhs - first * image + second * mapped_image]
    )
    out = lax.all_to_all(out, "dates", split_axis=1, concat_axis=3, tiled=True)
    return (out[0], out[1])


def solution(mesh):
    return jax.shard_map(
        body,
        mesh=mesh,
        in_specs=(
            P("dates", "rows", None),
            P("dates", "rows", None),
            P("dates", "rows", None),
            P(None, "rows", None),
            P(),
            P(None, None, "rows", "dates"),
        ),
        out_specs=(P("dates", "rows", None), P("dates", "rows", None)),
        check_vma=False,
    )
```

profile of v0, /device:TPU:26, one launch (start us, length us, event | category | flops | bytes accessed | tf_op | source)
XLA Modules:
  0.0 248.5 jit_solution(16082085440796772396)
XLA Ops:
  1.8 8.2 %copy.156 = f32[2,2,8,4096]{2,1,0,3:T(2,128)} copy(f32[2,2,8,4096]{3,2,1,0:T(8,128)S(1)} %pad_maximum_fusion) | data formatting | bytes 1048576 | tf_op jit(solution)/shard_map/stack | solution.py:29
  10.0 15.6 %reshape.805 = f32[8,1,16384]{2,1,0:T(1,128)} reshape(f32[4096,2,2,8]{3,2,1,0:T(2,128)} %bitcast.617) | data formatting | bytes 1048576
  25.7 10.4 %all-to-all-start = ((f32[8,1,16384]{2,1,0:T(1,128)}), f32[8,1,16384]{2,1,0:T(1,128)S(1)}, u32[]{:S(2)}, u32[]{:S(2)}) async-start(f32[8,1,16384]{2,1,0:T(1,128)} %reshape.805), calls=%async_computation | async-start | bytes 1048576 | tf_op jit(solution)/shard_map/all_to_all | solution.py:30
  36.3 2.1 collective-permute-start
  39.1 1.9 bitcast_convert_fusion.15
  42.4 11.2 %all-to-all-done = f32[8,1,16384]{2,1,0:T(1,128)S(1)} async-done(((f32[8,1,16384]{2,1,0:T(1,128)}), f32[8,1,16384]{2,1,0:T(1,128)S(1)}, u32[]{:S(2)}, u32[]{:S(2)}) %all-to-all-start) | async-done | bytes 524320 | tf_op jit(solution)/shard_map/all_to_all | solution.py:30
  54.1 1.9 reduce.1
  56.0 16.0 %reshape.806 = f32[4096,2,2,8]{3,2,1,0:T(2,128)} reshape(f32[8,16384]{1,0:T(8,128)S(1)} %reduce.1) | data formatting | bytes 1048576
  72.0 10.1 %copy.158 = f32[2,2,8,8,512]{4,2,1,3,0:T(8,128)S(1)} copy(f32[2,2,8,8,512]{2,1,0,4,3:T(2,128)} %bitcast.618) | data formatting | bytes 1048576 | tf_op jit(solution)/shard_map/all_to_all | solution.py:30
  83.1 1.4 collective-permute-start.1
  84.5 4.5 %collective-permute-start.2 = (f32[16,8,1]{2,1,0:T(8,128)S(1)}, f32[16,8,1]{2,1,0:T(8,128)S(1)}, u32[]{:S(2)}, u32[]{:S(2)}) collective-permute-start(f32[16,8,1]{2,1,0:T(8,128)S(1)} %get-tuple-element.60), channel_id=1, source_target_pairs={{0,1},{1,2},{2,3},{3,4},{4,5},{5,6},{6,7},{8,9},{9,10},{10,11},{11... | collective-permute-start | bytes 1544 | tf_op jit(solution)/shard_map/ppermute | solution.py:12
  89.1 1.9 collective-permute-start.3
  91.0 2.4 collective-permute-start.4
  93.6 1.2 multiply_reduce_fusion.3
  97.3 1.3 collective-permute-start.5
  98.6 4.5 %collective-permute-start.6 = (f32[16,8,1]{2,1,0:T(8,128)S(1)}, f32[16,8,1]{2,1,0:T(8,128)S(1)}, u32[]{:S(2)}, u32[]{:S(2)}) collective-permute-start(f32[16,8,1]{2,1,0:T(8,128)S(1)} %get-tuple-element.35), channel_id=1, source_target_pairs={{0,1},{1,2},{2,3},{3,4},{4,5},{5,6},{6,7},{8,9},{9,10},{10,11},{11... | collective-permute-start | bytes 1544 | tf_op jit(solution)/shard_map/ppermute | solution.py:12
  103.2 1.9 collective-permute-start.7
  105.1 2.6 %collective-permute-start.8 = (f32[16,1,512]{2,1,0:T(1,128)S(1)}, f32[16,1,512]{2,1,0:T(1,128)S(1)}, u32[]{:S(2)}, u32[]{:S(2)}) collective-permute-start(f32[16,1,512]{2,1,0:T(1,128)S(1)} %get-tuple-element.39), channel_id=1, source_target_pairs={{0,8},{8,16},{16,24},{24,32},{32,40},{40,48},{48,56},{56,64},{64,7... | collective-permute-start | bytes 98312 | tf_op jit(solution)/shard_map/ppermute | solution.py:12
  107.8 5.2 %collective-permute-done.8 = f32[16,1,512]{2,1,0:T(1,128)S(1)} collective-permute-done((f32[16,1,512]{2,1,0:T(1,128)S(1)}, f32[16,1,512]{2,1,0:T(1,128)S(1)}, u32[]{:S(2)}, u32[]{:S(2)}) %collective-permute-start.8) | collective-permute-done | bytes 32800 | tf_op jit(solution)/shard_map/ppermute | solution.py:12
  113.1 1.5 multiply_reduce_fusion.2
  114.6 2.6 %pad_maximum_fusion.5 = f32[4]{0:T(128)S(1)} fusion(f32[1]{0:T(128)} %bitcast.76, f32[1]{0:T(128)} %bitcast.75, f32[1]{0:T(128)} %bitcast.58, f32[1]{0:T(128)} %bitcast.37), kind=kLoop, calls=%fused_computation.229 | loop fusion | flops 12 | bytes 32 | tf_op jit(solution)/shard_map/stack | solution.py:70
  117.2 100.8 %psum.7 = f32[4]{0:T(128)S(1)} all-reduce(f32[4]{0:T(128)S(1)} %pad_maximum_fusion.5), channel_id=1, replica_groups=mesh['rows'=64,'dates'=8] {'rows','dates'}, use_global_device_ids=true, to_apply=%region_4.5 | all-reduce | flops 4 | bytes 32 | tf_op jit(solution)/shard_map/psum | solution.py:78
  225.1 1.6 fusion.19
  226.8 20.2 %all_to_all.30 = f32[2,16,8,512]{3,2,0,1:T(8,128)S(1)} all-to-all(f32[2,16,8,512]{3,2,0,1:T(8,128)S(1)} %pad_maximum_fusion.1), channel_id=1, replica_groups=mesh['rows'=64,'dates'=8] {'dates'}, dimensions={1} | all-to-all | bytes 1048576 | tf_op jit(solution)/shard_map/all_to_all | solution.py:88
  (107 shorter events, 9.3 us)
Async XLA Ops:
  10.0 26.1 %copy-start.23 = (s32[2,8,4096]{2,1,0:T(8,128)S(1)}, s32[2,8,4096]{2,1,0:T(8,128)}, u32[]{:S(2)}) copy-start(s32[2,8,4096]{2,1,0:T(8,128)} %param.9) | copy-start | bytes 786436
  25.7 13.4 %copy-start = (bf16[16,16,8,512]{3,2,1,0:T(8,128)(2,1)S(1)}, bf16[16,16,8,512]{3,2,1,0:T(8,128)(2,1)}, u32[]{:S(2)}) copy-start(bf16[16,16,8,512]{3,2,1,0:T(8,128)(2,1)} %param.11) | copy-start | bytes 6291460
  25.7 27.9 %all-to-all-start = ((f32[8,1,16384]{2,1,0:T(1,128)}), f32[8,1,16384]{2,1,0:T(1,128)S(1)}, u32[]{:S(2)}, u32[]{:S(2)}) async-start(f32[8,1,16384]{2,1,0:T(1,128)} %reshape.805), calls=%async_computation | async-start | bytes 1048576 | tf_op jit(solution)/shard_map/all_to_all | solution.py:30
  36.3 5.4 %collective-permute-start = (f32[1,512]{1,0:T(1,128)S(1)}, f32[1,512]{1,0:T(1,128)S(1)}, u32[]{:S(2)}, u32[]{:S(2)}) collective-permute-start(f32[1,512]{1,0:T(1,128)S(1)} %slice.360), channel_id=1, source_target_pairs={{0,8},{8,16},{16,24},{24,32},{32,40},{40,48},{48,56},{56,64},{64,7... | collective-permute-start | bytes 6152 | tf_op jit(solution)/shard_map/ppermute | solution.py:12
  82.2 30.8 %copy-start.16 = (f32[8,512]{1,0:T(8,128)}, f32[8,512]{1,0:T(8,128)S(1)}, u32[]{:S(2)}) copy-start(f32[8,512]{1,0:T(8,128)S(1)} %get-tuple-element.73) | copy-start | bytes 49156
  82.2 30.8 %copy-start.17 = (f32[8,512]{1,0:T(8,128)}, f32[8,512]{1,0:T(8,128)S(1)}, u32[]{:S(2)}) copy-start(f32[8,512]{1,0:T(8,128)S(1)} %get-tuple-element.74) | copy-start | bytes 49156
  82.2 30.8 %copy-start.18 = (f32[8,512]{1,0:T(8,128)}, f32[8,512]{1,0:T(8,128)S(1)}, u32[]{:S(2)}) copy-start(f32[8,512]{1,0:T(8,128)S(1)} %get-tuple-element.75) | copy-start | bytes 49156
  82.3 30.8 %copy-start.19 = (f32[8,512]{1,0:T(8,128)}, f32[8,512]{1,0:T(8,128)S(1)}, u32[]{:S(2)}) copy-start(f32[8,512]{1,0:T(8,128)S(1)} %get-tuple-element.76) | copy-start | bytes 49156
  82.3 30.8 %copy-start.20 = (f32[8,512]{1,0:T(8,128)}, f32[8,512]{1,0:T(8,128)S(1)}, u32[]{:S(2)}) copy-start(f32[8,512]{1,0:T(8,128)S(1)} %get-tuple-element.77) | copy-start | bytes 49156
  82.3 30.8 %copy-start.21 = (f32[8,512]{1,0:T(8,128)}, f32[8,512]{1,0:T(8,128)S(1)}, u32[]{:S(2)}) copy-start(f32[8,512]{1,0:T(8,128)S(1)} %get-tuple-element.78) | copy-start | bytes 49156
  82.3 30.8 %copy-start.22 = (f32[8,512]{1,0:T(8,128)}, f32[8,512]{1,0:T(8,128)S(1)}, u32[]{:S(2)}) copy-start(f32[8,512]{1,0:T(8,128)S(1)} %get-tuple-element.79) | copy-start | bytes 49156
  82.3 11.1 %copy-start.1 = (f32[16,1,8,512]{3,2,0,1:T(8,128)S(1)}, f32[16,1,8,512]{3,2,0,1:T(8,128)}, u32[]{:S(2)}) copy-start(f32[16,1,8,512]{3,2,0,1:T(8,128)} %get-tuple-element.11) | copy-start | bytes 786436
  82.3 11.1 %copy-start.2 = (f32[16,1,8,512]{3,2,0,1:T(8,128)S(1)}, f32[16,1,8,512]{3,2,0,1:T(8,128)}, u32[]{:S(2)}) copy-start(f32[16,1,8,512]{3,2,0,1:T(8,128)} %get-tuple-element.12) | copy-start | bytes 786436
  82.3 11.1 %copy-start.3 = (f32[16,1,8,512]{3,2,0,1:T(8,128)S(1)}, f32[16,1,8,512]{3,2,0,1:T(8,128)}, u32[]{:S(2)}) copy-start(f32[16,1,8,512]{3,2,0,1:T(8,128)} %get-tuple-element.13) | copy-start | bytes 786436
  82.3 11.1 %copy-start.4 = (f32[16,1,8,512]{3,2,0,1:T(8,128)S(1)}, f32[16,1,8,512]{3,2,0,1:T(8,128)}, u32[]{:S(2)}) copy-start(f32[16,1,8,512]{3,2,0,1:T(8,128)} %get-tuple-element.14) | copy-start | bytes 786436
  82.3 11.1 %copy-start.5 = (f32[16,1,8,512]{3,2,0,1:T(8,128)S(1)}, f32[16,1,8,512]{3,2,0,1:T(8,128)}, u32[]{:S(2)}) copy-start(f32[16,1,8,512]{3,2,0,1:T(8,128)} %get-tuple-element.15) | copy-start | bytes 786436
  83.1 11.9 %collective-permute-start.1 = (f32[16,8,1]{2,1,0:T(8,128)S(1)}, f32[16,8,1]{2,1,0:T(8,128)S(1)}, u32[]{:S(2)}, u32[]{:S(2)}) collective-permute-start(f32[16,8,1]{2,1,0:T(8,128)S(1)} %get-tuple-element.61), channel_id=1, source_target_pairs={{1,0},{2,1},{3,2},{4,3},{5,4},{6,5},{7,6},{9,8},{10,9},{11,10},{12... | collective-permute-start | bytes 1544 | tf_op jit(solution)/shard_map/ppermute | solution.py:12
  84.5 10.5 %collective-permute-start.2 = (f32[16,8,1]{2,1,0:T(8,128)S(1)}, f32[16,8,1]{2,1,0:T(8,128)S(1)}, u32[]{:S(2)}, u32[]{:S(2)}) collective-permute-start(f32[16,8,1]{2,1,0:T(8,128)S(1)} %get-tuple-element.60), channel_id=1, source_target_pairs={{0,1},{1,2},{2,3},{3,4},{4,5},{5,6},{6,7},{8,9},{9,10},{10,11},{11... | collective-permute-start | bytes 1544 | tf_op jit(solution)/shard_map/ppermute | solution.py:12
  89.1 6.0 %collective-permute-start.3 = (f32[16,1,512]{2,1,0:T(1,128)S(1)}, f32[16,1,512]{2,1,0:T(1,128)S(1)}, u32[]{:S(2)}, u32[]{:S(2)}) collective-permute-start(f32[16,1,512]{2,1,0:T(1,128)S(1)} %get-tuple-element.57), channel_id=1, source_target_pairs={{8,0},{16,8},{24,16},{32,24},{40,32},{48,40},{56,48},{64,56},{72,6... | collective-permute-start | bytes 98312 | tf_op jit(solution)/shard_map/ppermute | solution.py:12
  91.0 5.2 %collective-permute-start.4 = (f32[16,1,512]{2,1,0:T(1,128)S(1)}, f32[16,1,512]{2,1,0:T(1,128)S(1)}, u32[]{:S(2)}, u32[]{:S(2)}) collective-permute-start(f32[16,1,512]{2,1,0:T(1,128)S(1)} %get-tuple-element.56), channel_id=1, source_target_pairs={{0,8},{8,16},{16,24},{24,32},{32,40},{40,48},{48,56},{56,64},{64,7... | collective-permute-start | bytes 98312 | tf_op jit(solution)/shard_map/ppermute | solution.py:12
  97.3 10.5 %collective-permute-start.5 = (f32[16,8,1]{2,1,0:T(8,128)S(1)}, f32[16,8,1]{2,1,0:T(8,128)S(1)}, u32[]{:S(2)}, u32[]{:S(2)}) collective-permute-start(f32[16,8,1]{2,1,0:T(8,128)S(1)} %get-tuple-element.34), channel_id=1, source_target_pairs={{1,0},{2,1},{3,2},{4,3},{5,4},{6,5},{7,6},{9,8},{10,9},{11,10},{12... | collective-permute-start | bytes 1544 | tf_op jit(solution)/shard_map/ppermute | solution.py:12
  98.6 9.2 %collective-permute-start.6 = (f32[16,8,1]{2,1,0:T(8,128)S(1)}, f32[16,8,1]{2,1,0:T(8,128)S(1)}, u32[]{:S(2)}, u32[]{:S(2)}) collective-permute-start(f32[16,8,1]{2,1,0:T(8,128)S(1)} %get-tuple-element.35), channel_id=1, source_target_pairs={{0,1},{1,2},{2,3},{3,4},{4,5},{5,6},{6,7},{8,9},{9,10},{10,11},{11... | collective-permute-start | bytes 1544 | tf_op jit(solution)/shard_map/ppermute | solution.py:12
  103.2 4.6 %collective-permute-start.7 = (f32[16,1,512]{2,1,0:T(1,128)S(1)}, f32[16,1,512]{2,1,0:T(1,128)S(1)}, u32[]{:S(2)}, u32[]{:S(2)}) collective-permute-start(f32[16,1,512]{2,1,0:T(1,128)S(1)} %get-tuple-element.38), channel_id=1, source_target_pairs={{8,0},{16,8},{24,16},{32,24},{40,32},{48,40},{56,48},{64,56},{72,6... | collective-permute-start | bytes 98312 | tf_op jit(solution)/shard_map/ppermute | solution.py:12
  105.1 7.9 %collective-permute-start.8 = (f32[16,1,512]{2,1,0:T(1,128)S(1)}, f32[16,1,512]{2,1,0:T(1,128)S(1)}, u32[]{:S(2)}, u32[]{:S(2)}) collective-permute-start(f32[16,1,512]{2,1,0:T(1,128)S(1)} %get-tuple-element.39), channel_id=1, source_target_pairs={{0,8},{8,16},{16,24},{24,32},{32,40},{40,48},{48,56},{56,64},{64,7... | collective-permute-start | bytes 98312 | tf_op jit(solution)/shard_map/ppermute | solution.py:12
  (19 other events, 134.2 us)
where the time goes:
time: 249 us; the launch traced here: 248 us
  blocking collectives  121 us (49%)
  local copies, waits for them, and re-layouts  53.4 us (21%)
  starting transfers between devices  33.2 us (13%)
  waiting for transfers between devices  17.6 us (7%)
  other arithmetic  15.4 us (6%)
  between operations  7.91 us (3%)
    psum x1, blocking collectives, body(): sums = lax.psum(sums, ('rows', 'dates'))  101 us
    unnamed x68, local copies, waits for them, and re-layouts  31.8 us
    ppermute x9, starting transfers between devices, shifted(): lax.ppermute(value, axis, [(i, i + steps) for i in range(first, last)])  22.8 us
    all_to_all x1, blocking collectives, body(): out = lax.all_to_all(out, 'dates', split_axis=1, concat_axis=3, tiled=True)  20.2 us
    all_to_all x1, waiting for transfers between devices, body(): lax.all_to_all(both, 'dates', split_axis=3, concat_axis=1, tiled=True)  11.2 us
    all_to_all x2, local copies, waits for them, and re-layouts, body(): lax.all_to_all(both, 'dates', split_axis=3, concat_axis=1, tiled=True)  10.6 us
    all_to_all x1, starting transfers between devices, body(): lax.all_to_all(both, 'dates', split_axis=3, concat_axis=1, tiled=True)  10.4 us
    another operation x1, local copies, waits for them, and re-layouts, body(): both = jnp.stack([weight, weight * observed])  8.2 us
  transfers between devices with their start and end apart: 10, of which 3 were waited for; matrix products, arithmetic and copies ran while one was open for 2% of the time, Pallas kernels for 0%

commit v1 on v0

--- a/solution.py
+++ b/solution.py
@@ -27,7 +27,10 @@
     col_start = lax.axis_index("dates") * cols_here
     weight = obs_mask.astype(jnp.float32) * precision
     both = jnp.stack([weight, weight * observed])
-    both = lax.all_to_all(both, "dates", split_axis=3, concat_axis=1, tiled=True)
+    both = jnp.concatenate(
+        lax.all_to_all(jnp.stack(jnp.split(both, lax.axis_size("dates"), axis=3)), "dates", 0, 0),
+        axis=1,
+    )
     weight, rhs = (both[0], both[1])
     classes = 0.25 * (edge_class.astype(jnp.float32) + 1.0)
     col_ids = lax.broadcasted_iota(jnp.int32, (rows_here, columns), 1)

time: 249 us -> 202 us (0.81)
  local copies, waits for them, and re-layouts: 53.4 us -> 3.48 us
  other arithmetic: 15.4 us -> 19.2 us
    unnamed x68 -> x70, local copies, waits for them, and re-layouts: 31.8 us -> 0.15 us
    all_to_all x2 -> x0, local copies, waits for them, and re-layouts: 10.6 us -> none  [body(): lax.all_to_all(both, 'dates', split_axis=3, concat_axis=1, tiled=True)]
    another operation x1 -> x0, local copies, waits for them, and re-layouts: 8.2 us -> none  [body(): both = jnp.stack([weight, weight * observed])]
    unnamed x0 -> x7, other arithmetic: none -> 4.39 us
  transfers between devices with their start and end apart: 10 -> 10, of which waited for: 3 -> 3; matrix products, arithmetic and copies ran while one was open for 2% -> 3% of each run, Pallas kernels for 0% -> 0%
where the time goes in v1:
time: 202 us; the launch traced here: 201 us
  blocking collectives  121 us (60%)
  starting transfers between devices  32.7 us (16%)
  other arithmetic  19.2 us (10%)
  waiting for transfers between devices  16.8 us (8%)
  between operations  7.91 us (4%)
  local copies, waits for them, and re-layouts  3.48 us (2%)
    psum x1, blocking collectives, body(): sums = lax.psum(sums, ('rows', 'dates'))  101 us
    ppermute x9, starting transfers between devices, shifted(): lax.ppermute(value, axis, [(i, i + steps) for i in range(first, last)])  22.4 us
    all_to_all x1, blocking collectives, body(): out = lax.all_to_all(out, 'dates', split_axis=1, concat_axis=3, tiled=True)  20.2 us
    all_to_all x1, starting transfers between devices, body(): lax.all_to_all(jnp.stack(jnp.split(both, lax.axis_size('dates'), axis=3))...  10.3 us
    all_to_all x1, waiting for transfers between devices, body(): lax.all_to_all(jnp.stack(jnp.split(both, lax.axis_size('dates'), axis=3))...  10.1 us
    ppermute x9, waiting for transfers between devices, shifted(): lax.ppermute(value, axis, [(i, i + steps) for i in range(first, last)])  6.66 us
    unnamed x7, other arithmetic  4.39 us
  transfers between devices with their start and end apart: 10, of which 3 were waited for; matrix products, arithmetic and copies ran while one was open for 3% of the time, Pallas kernels for 0%

profile of v1, /device:TPU:26, one launch (start us, length us, event | category | flops | bytes accessed | tf_op | source)
XLA Modules:
  0.0 200.9 jit_solution(10754184155584990792)
XLA Ops:
  0.6 1.2 multiply_bitcast_fusion
  6.8 10.3 %all-to-all-start = ((f32[8,2,2,8,512]{4,3,2,1,0:T(8,128)}), f32[8,2,2,8,512]{4,3,2,1,0:T(8,128)S(1)}, u32[]{:S(2)}, u32[]{:S(2)}) async-start(f32[8,2,2,8,512]{4,3,2,1,0:T(8,128)} %fusion.105), calls=%async_computation | async-start | bytes 1048576 | tf_op jit(solution)/shard_map/all_to_all | solution.py:31
  17.9 1.9 collective-permute-start
  20.5 1.8 bitcast_convert_fusion.15
  23.1 1.4 add_add_fusion
  24.5 10.1 %all-to-all-done = f32[8,2,2,8,512]{4,3,2,1,0:T(8,128)S(1)} async-done(((f32[8,2,2,8,512]{4,3,2,1,0:T(8,128)}), f32[8,2,2,8,512]{4,3,2,1,0:T(8,128)S(1)}, u32[]{:S(2)}, u32[]{:S(2)}) %all-to-all-start) | async-done | bytes 524320 | tf_op jit(solution)/shard_map/all_to_all | solution.py:31
  35.5 1.4 collective-permute-start.1
  37.0 4.5 %collective-permute-start.2 = (f32[16,8,1]{2,1,0:T(8,128)S(1)}, f32[16,8,1]{2,1,0:T(8,128)S(1)}, u32[]{:S(2)}, u32[]{:S(2)}) collective-permute-start(f32[16,8,1]{2,1,0:T(8,128)S(1)} %get-tuple-element.60), channel_id=1, source_target_pairs={{0,1},{1,2},{2,3},{3,4},{4,5},{5,6},{6,7},{8,9},{9,10},{10,11},{11... | collective-permute-start | bytes 1544 | tf_op jit(solution)/shard_map/ppermute | solution.py:12
  41.5 1.9 collective-permute-start.3
  43.4 2.4 %collective-permute-start.4 = (f32[16,1,512]{2,1,0:T(1,128)S(1)}, f32[16,1,512]{2,1,0:T(1,128)S(1)}, u32[]{:S(2)}, u32[]{:S(2)}) collective-permute-start(f32[16,1,512]{2,1,0:T(1,128)S(1)} %get-tuple-element.56), channel_id=1, source_target_pairs={{0,8},{8,16},{16,24},{24,32},{32,40},{40,48},{48,56},{56,64},{64,7... | collective-permute-start | bytes 98312 | tf_op jit(solution)/shard_map/ppermute | solution.py:12
  46.1 1.3 multiply_reduce_fusion.3
  47.5 1.2 collective-permute-done.4
  49.8 1.3 collective-permute-start.5
  51.1 4.5 %collective-permute-start.6 = (f32[16,8,1]{2,1,0:T(8,128)S(1)}, f32[16,8,1]{2,1,0:T(8,128)S(1)}, u32[]{:S(2)}, u32[]{:S(2)}) collective-permute-start(f32[16,8,1]{2,1,0:T(8,128)S(1)} %get-tuple-element.35), channel_id=1, source_target_pairs={{0,1},{1,2},{2,3},{3,4},{4,5},{5,6},{6,7},{8,9},{9,10},{10,11},{11... | collective-permute-start | bytes 1544 | tf_op jit(solution)/shard_map/ppermute | solution.py:12
  55.6 1.9 collective-permute-start.7
  57.6 2.4 %collective-permute-start.8 = (f32[16,1,512]{2,1,0:T(1,128)S(1)}, f32[16,1,512]{2,1,0:T(1,128)S(1)}, u32[]{:S(2)}, u32[]{:S(2)}) collective-permute-start(f32[16,1,512]{2,1,0:T(1,128)S(1)} %get-tuple-element.39), channel_id=1, source_target_pairs={{0,8},{8,16},{16,24},{24,32},{32,40},{40,48},{48,56},{56,64},{64,7... | collective-permute-start | bytes 98312 | tf_op jit(solution)/shard_map/ppermute | solution.py:12
  60.1 5.4 %collective-permute-done.8 = f32[16,1,512]{2,1,0:T(1,128)S(1)} collective-permute-done((f32[16,1,512]{2,1,0:T(1,128)S(1)}, f32[16,1,512]{2,1,0:T(1,128)S(1)}, u32[]{:S(2)}, u32[]{:S(2)}) %collective-permute-start.8) | collective-permute-done | bytes 32800 | tf_op jit(solution)/shard_map/ppermute | solution.py:12
  65.6 1.5 multiply_reduce_fusion.2
  67.0 2.7 %pad_maximum_fusion.5 = f32[4]{0:T(128)S(1)} fusion(f32[1]{0:T(128)} %bitcast.99, f32[1]{0:T(128)} %bitcast.98, f32[1]{0:T(128)} %bitcast.81, f32[1]{0:T(128)} %bitcast.60), kind=kLoop, calls=%fused_computation.266 | loop fusion | flops 12 | bytes 32 | tf_op jit(solution)/shard_map/stack | solution.py:73
  69.7 100.7 %psum.7 = f32[4]{0:T(128)S(1)} all-reduce(f32[4]{0:T(128)S(1)} %pad_maximum_fusion.5), channel_id=1, replica_groups=mesh['rows'=64,'dates'=8] {'rows','dates'}, use_global_device_ids=true, to_apply=%region_4.5 | all-reduce | flops 4 | bytes 32 | tf_op jit(solution)/shard_map/psum | solution.py:81
  177.6 1.6 fusion.19
  179.3 20.2 %all_to_all.20 = f32[2,16,8,512]{3,2,0,1:T(8,128)S(1)} all-to-all(f32[2,16,8,512]{3,2,0,1:T(8,128)S(1)} %pad_maximum_fusion), channel_id=1, replica_groups=mesh['rows'=64,'dates'=8] {'dates'}, dimensions={1} | all-to-all | bytes 1048576 | tf_op jit(solution)/shard_map/all_to_all | solution.py:91
  199.5 0.7 copy.73
  200.2 0.7 copy.74
  (112 shorter events, 9.9 us)
Async XLA Ops:
  3.7 13.5 %copy-start.22 = (s32[2,8,4096]{2,1,0:T(8,128)S(1)}, s32[2,8,4096]{2,1,0:T(8,128)}, u32[]{:S(2)}) copy-start(s32[2,8,4096]{2,1,0:T(8,128)} %param.9) | copy-start | bytes 786436
  4.9 15.6 %copy-start = (bf16[16,16,8,512]{3,2,1,0:T(8,128)(2,1)S(1)}, bf16[16,16,8,512]{3,2,1,0:T(8,128)(2,1)}, u32[]{:S(2)}) copy-start(bf16[16,16,8,512]{3,2,1,0:T(8,128)(2,1)} %param.11) | copy-start | bytes 6291460
  6.8 27.8 %all-to-all-start = ((f32[8,2,2,8,512]{4,3,2,1,0:T(8,128)}), f32[8,2,2,8,512]{4,3,2,1,0:T(8,128)S(1)}, u32[]{:S(2)}, u32[]{:S(2)}) async-start(f32[8,2,2,8,512]{4,3,2,1,0:T(8,128)} %fusion.105), calls=%async_computation | async-start | bytes 1048576 | tf_op jit(solution)/shard_map/all_to_all | solution.py:31
  17.9 5.2 %collective-permute-start = (f32[1,512]{1,0:T(1,128)}, f32[1,512]{1,0:T(1,128)}, u32[]{:S(2)}, u32[]{:S(2)}) collective-permute-start(f32[1,512]{1,0:T(1,128)} %slice.360), channel_id=1, source_target_pairs={{0,8},{8,16},{16,24},{24,32},{32,40},{40,48},{48,56},{56,64},{64,7... | collective-permute-start | bytes 6152 | tf_op jit(solution)/shard_map/ppermute | solution.py:12
  34.7 30.8 %copy-start.15 = (f32[8,512]{1,0:T(8,128)}, f32[8,512]{1,0:T(8,128)S(1)}, u32[]{:S(2)}) copy-start(f32[8,512]{1,0:T(8,128)S(1)} %get-tuple-element.73) | copy-start | bytes 49156
  34.7 30.8 %copy-start.16 = (f32[8,512]{1,0:T(8,128)}, f32[8,512]{1,0:T(8,128)S(1)}, u32[]{:S(2)}) copy-start(f32[8,512]{1,0:T(8,128)S(1)} %get-tuple-element.74) | copy-start | bytes 49156
  34.7 30.8 %copy-start.17 = (f32[8,512]{1,0:T(8,128)}, f32[8,512]{1,0:T(8,128)S(1)}, u32[]{:S(2)}) copy-start(f32[8,512]{1,0:T(8,128)S(1)} %get-tuple-element.75) | copy-start | bytes 49156
  34.7 30.8 %copy-start.18 = (f32[8,512]{1,0:T(8,128)}, f32[8,512]{1,0:T(8,128)S(1)}, u32[]{:S(2)}) copy-start(f32[8,512]{1,0:T(8,128)S(1)} %get-tuple-element.76) | copy-start | bytes 49156
  34.7 30.8 %copy-start.19 = (f32[8,512]{1,0:T(8,128)}, f32[8,512]{1,0:T(8,128)S(1)}, u32[]{:S(2)}) copy-start(f32[8,512]{1,0:T(8,128)S(1)} %get-tuple-element.77) | copy-start | bytes 49156
  34.7 30.8 %copy-start.20 = (f32[8,512]{1,0:T(8,128)}, f32[8,512]{1,0:T(8,128)S(1)}, u32[]{:S(2)}) copy-start(f32[8,512]{1,0:T(8,128)S(1)} %get-tuple-element.78) | copy-start | bytes 49156
  34.8 30.8 %copy-start.21 = (f32[8,512]{1,0:T(8,128)}, f32[8,512]{1,0:T(8,128)S(1)}, u32[]{:S(2)}) copy-start(f32[8,512]{1,0:T(8,128)S(1)} %get-tuple-element.79) | copy-start | bytes 49156
  34.8 11.1 %copy-start.1 = (f32[16,1,8,512]{3,2,0,1:T(8,128)S(1)}, f32[16,1,8,512]{3,2,0,1:T(8,128)}, u32[]{:S(2)}) copy-start(f32[16,1,8,512]{3,2,0,1:T(8,128)} %get-tuple-element.12) | copy-start | bytes 786436
  34.8 11.1 %copy-start.2 = (f32[16,1,8,512]{3,2,0,1:T(8,128)S(1)}, f32[16,1,8,512]{3,2,0,1:T(8,128)}, u32[]{:S(2)}) copy-start(f32[16,1,8,512]{3,2,0,1:T(8,128)} %get-tuple-element.13) | copy-start | bytes 786436
  34.8 11.1 %copy-start.3 = (f32[16,1,8,512]{3,2,0,1:T(8,128)S(1)}, f32[16,1,8,512]{3,2,0,1:T(8,128)}, u32[]{:S(2)}) copy-start(f32[16,1,8,512]{3,2,0,1:T(8,128)} %get-tuple-element.14) | copy-start | bytes 786436
  34.8 11.1 %copy-start.4 = (f32[16,1,8,512]{3,2,0,1:T(8,128)S(1)}, f32[16,1,8,512]{3,2,0,1:T(8,128)}, u32[]{:S(2)}) copy-start(f32[16,1,8,512]{3,2,0,1:T(8,128)} %get-tuple-element.15) | copy-start | bytes 786436
  34.8 11.1 %copy-start.5 = (f32[16,1,8,512]{3,2,0,1:T(8,128)S(1)}, f32[16,1,8,512]{3,2,0,1:T(8,128)}, u32[]{:S(2)}) copy-start(f32[16,1,8,512]{3,2,0,1:T(8,128)} %get-tuple-element.16) | copy-start | bytes 786436
  35.5 12.0 %collective-permute-start.1 = (f32[16,8,1]{2,1,0:T(8,128)S(1)}, f32[16,8,1]{2,1,0:T(8,128)S(1)}, u32[]{:S(2)}, u32[]{:S(2)}) collective-permute-start(f32[16,8,1]{2,1,0:T(8,128)S(1)} %get-tuple-element.61), channel_id=1, source_target_pairs={{1,0},{2,1},{3,2},{4,3},{5,4},{6,5},{7,6},{9,8},{10,9},{11,10},{12... | collective-permute-start | bytes 1544 | tf_op jit(solution)/shard_map/ppermute | solution.py:12
  37.0 10.5 %collective-permute-start.2 = (f32[16,8,1]{2,1,0:T(8,128)S(1)}, f32[16,8,1]{2,1,0:T(8,128)S(1)}, u32[]{:S(2)}, u32[]{:S(2)}) collective-permute-start(f32[16,8,1]{2,1,0:T(8,128)S(1)} %get-tuple-element.60), channel_id=1, source_target_pairs={{0,1},{1,2},{2,3},{3,4},{4,5},{5,6},{6,7},{8,9},{9,10},{10,11},{11... | collective-permute-start | bytes 1544 | tf_op jit(solution)/shard_map/ppermute | solution.py:12
  41.5 6.0 %collective-permute-start.3 = (f32[16,1,512]{2,1,0:T(1,128)S(1)}, f32[16,1,512]{2,1,0:T(1,128)S(1)}, u32[]{:S(2)}, u32[]{:S(2)}) collective-permute-start(f32[16,1,512]{2,1,0:T(1,128)S(1)} %get-tuple-element.57), channel_id=1, source_target_pairs={{8,0},{16,8},{24,16},{32,24},{40,32},{48,40},{56,48},{64,56},{72,6... | collective-permute-start | bytes 98312 | tf_op jit(solution)/shard_map/ppermute | solution.py:12
  43.4 5.2 %collective-permute-start.4 = (f32[16,1,512]{2,1,0:T(1,128)S(1)}, f32[16,1,512]{2,1,0:T(1,128)S(1)}, u32[]{:S(2)}, u32[]{:S(2)}) collective-permute-start(f32[16,1,512]{2,1,0:T(1,128)S(1)} %get-tuple-element.56), channel_id=1, source_target_pairs={{0,8},{8,16},{16,24},{24,32},{32,40},{40,48},{48,56},{56,64},{64,7... | collective-permute-start | bytes 98312 | tf_op jit(solution)/shard_map/ppermute | solution.py:12
  49.8 10.3 %collective-permute-start.5 = (f32[16,8,1]{2,1,0:T(8,128)S(1)}, f32[16,8,1]{2,1,0:T(8,128)S(1)}, u32[]{:S(2)}, u32[]{:S(2)}) collective-permute-start(f32[16,8,1]{2,1,0:T(8,128)S(1)} %get-tuple-element.34), channel_id=1, source_target_pairs={{1,0},{2,1},{3,2},{4,3},{5,4},{6,5},{7,6},{9,8},{10,9},{11,10},{12... | collective-permute-start | bytes 1544 | tf_op jit(solution)/shard_map/ppermute | solution.py:12
  51.1 9.0 %collective-permute-start.6 = (f32[16,8,1]{2,1,0:T(8,128)S(1)}, f32[16,8,1]{2,1,0:T(8,128)S(1)}, u32[]{:S(2)}, u32[]{:S(2)}) collective-permute-start(f32[16,8,1]{2,1,0:T(8,128)S(1)} %get-tuple-element.35), channel_id=1, source_target_pairs={{0,1},{1,2},{2,3},{3,4},{4,5},{5,6},{6,7},{8,9},{9,10},{10,11},{11... | collective-permute-start | bytes 1544 | tf_op jit(solution)/shard_map/ppermute | solution.py:12
  55.6 4.4 %collective-permute-start.7 = (f32[16,1,512]{2,1,0:T(1,128)S(1)}, f32[16,1,512]{2,1,0:T(1,128)S(1)}, u32[]{:S(2)}, u32[]{:S(2)}) collective-permute-start(f32[16,1,512]{2,1,0:T(1,128)S(1)} %get-tuple-element.38), channel_id=1, source_target_pairs={{8,0},{16,8},{24,16},{32,24},{40,32},{48,40},{56,48},{64,56},{72,6... | collective-permute-start | bytes 98312 | tf_op jit(solution)/shard_map/ppermute | solution.py:12
  57.6 7.9 %collective-permute-start.8 = (f32[16,1,512]{2,1,0:T(1,128)S(1)}, f32[16,1,512]{2,1,0:T(1,128)S(1)}, u32[]{:S(2)}, u32[]{:S(2)}) collective-permute-start(f32[16,1,512]{2,1,0:T(1,128)S(1)} %get-tuple-element.39), channel_id=1, source_target_pairs={{0,8},{8,16},{16,24},{24,32},{32,40},{40,48},{48,56},{56,64},{64,7... | collective-permute-start | bytes 98312 | tf_op jit(solution)/shard_map/ppermute | solution.py:12
  (21 other events, 130.8 us)
